TPU v7x, 32 devices: a whole 2x2x4 slice. The times are simulated.
32 devices in a mesh: row: 2 (over x), col: 8 (over z, y), layer: 2 (over core).
Axes of the slice: x: 2, y: 2, z: 4, core: 2. Of those that a mesh axis runs over, the one named last changes fastest.
Arguments:
- owned_blocks: bfloat16 [512, 32, 128, 128], P(('row', 'col', 'layer')), may hold values from -1 to 1
- slot_rows: int32 [512], P(('row', 'col', 'layer')), may hold values from -1 to 255, as said below
- block_cols: int32 [512, 32], P(('row', 'col', 'layer')), may hold values from 0 to 255, as said below
Outputs:
- product_blocks: bfloat16 [256, 32, 128, 128], P(('row', 'layer'), 'col')
Inputs may be any that keep to these rules, and one draw needn't show every extreme that they name: `slot_rows`: every block row appears in exactly one slot. The 16 slots of the device at grid row r, grid column c and layer l (slots ((r * 8 + c) * 2 + l) * 16 onward) hold only block rows i with i // 128 = r and (i // 16) % 2 = l, or -1. In every grid row and layer some device uses all of its slots. block_cols[s, p] lies in panel p, between p * 8 and p * 8 + 7, also for unused slots.
All inputs are finite; a program needn't handle non-finite values.
Results may differ from a plain program's by a relative error of at most 0.001.
Values may be sent and summed in bfloat16 or wider, within the bound.
A program may use at most 256 MiB of HBM per device.

v0:
```python
import jax
import jax.numpy as jnp
from jax import lax
from jax.sharding import PartitionSpec as P

NB = 256


def grid_positions(row_ids, panels, panel_width, grid_row, rows_grid, layers, per_device):
    panel_index = row_ids // panel_width
    offset = row_ids % panel_width
    local_panel = panel_index - grid_row * (panels // rows_grid)
    layer_of = panel_index // per_device % layers
    half_rows = panels // rows_grid * panel_width // layers
    within = (
        local_panel // (per_device * layers) * per_device + local_panel % per_device
    ) * panel_width + offset
    placed = layer_of * half_rows + within
    return jnp.where(row_ids >= 0, placed, layers * half_rows).astype(jnp.int32)


def shards(owned_blocks, slot_rows, block_cols):
    own_slots = owned_blocks.shape[0]
    panels = owned_blocks.shape[1]
    block_size = owned_blocks.shape[2]
    rows_grid = lax.axis_size("row")
    cols_grid = lax.axis_size("col")
    layers = lax.axis_size("layer")
    per_device = panels // (cols_grid * layers)
    panel_width = NB // panels
    tile_rows = NB // rows_grid
    slots_here = layers * per_device
    outgoing = (
        owned_blocks.reshape(own_slots, cols_grid * layers, per_device, block_size, block_size),
        block_cols.reshape(own_slots, cols_grid * layers, per_device),
        jnp.broadcast_to(slot_rows[:, None], (own_slots, cols_grid * layers)),
        jnp.broadcast_to(block_cols[:, None, :], (own_slots, cols_grid * layers, panels)),
    )
    got_blocks, got_cols, got_rows, got_every = (
        lax.all_to_all(outgoing[0], ("col", "layer"), split_axis=1, concat_axis=0, tiled=True),
        lax.all_to_all(outgoing[1], ("col", "layer"), split_axis=1, concat_axis=0, tiled=True),
        lax.all_to_all(outgoing[2], ("col", "layer"), split_axis=1, concat_axis=0, tiled=True),
        lax.all_to_all(outgoing[3], ("col", "layer"), split_axis=1, concat_axis=0, tiled=True),
    )
    got_rows = got_rows.reshape(-1)
    slot_total = got_rows.shape[0]
    got_blocks = got_blocks.reshape(slot_total, per_device, block_size, block_size)
    got_cols = got_cols.reshape(slot_total, per_device)
    got_every = got_every.reshape(slot_total, panels)
    target = grid_positions(
        got_rows, panels, panel_width, lax.axis_index("row"), rows_grid, layers, per_device
    )
    row_tile = (
        jnp.zeros((tile_rows, per_device, block_size, block_size), jnp.bfloat16)
        .at[target]
        .set(got_blocks, mode="drop")
    )
    col_tile = jnp.zeros((tile_rows, per_device), jnp.int32).at[target].set(got_cols, mode="drop")
    every_cols = jnp.zeros((tile_rows, panels), jnp.int32).at[target].set(got_every, mode="drop")
    target_cols = lax.dynamic_slice_in_dim(
        every_cols, lax.axis_index("col") * slots_here, slots_here, 1
    )
    column_tile, column_ids = (
        lax.all_to_all(row_tile, "layer", split_axis=0, concat_axis=1, tiled=True),
        lax.all_to_all(col_tile, "layer", split_axis=0, concat_axis=1, tiled=True),
    )
    column_table, column_ids = (
        lax.all_gather(column_tile, "row", axis=0, tiled=True),
        lax.all_gather(column_ids, "row", axis=0, tiled=True),
    )
    column_table = column_table.reshape(
        panels // layers, panel_width, slots_here, block_size, block_size
    )
    column_ids = column_ids.reshape(panels // layers, panel_width, slots_here)
    initial = jnp.zeros((tile_rows, slots_here, block_size, block_size), jnp.float32)
    piece_blocks = lax.all_gather(row_tile, "col", axis=1, tiled=True)
    piece_cols = lax.all_gather(col_tile, "col", axis=1, tiled=True)
    panel_count = piece_blocks.shape[1]
    panel_steps = jnp.arange(panel_count, dtype=jnp.int32)
    offsets = piece_cols % panel_width

    def one_block(block_index):
        left_blocks = lax.dynamic_slice_in_dim(piece_blocks, block_index * 8, 8, 0)
        row_offsets = lax.dynamic_slice_in_dim(offsets, block_index * 8, 8, 0)
        wanted = lax.dynamic_slice_in_dim(target_cols, block_index * 8, 8, 0)
        chosen = column_table[panel_steps[None, :], row_offsets]
        chosen_ids = column_ids[panel_steps[None, :], row_offsets]
        matched = chosen_ids == wanted[:, None, :]
        chosen = jnp.where(matched[:, :, :, None, None], chosen, jnp.zeros((), jnp.bfloat16))
        return jnp.einsum(
            "mtab,mtsbc->msac", left_blocks, chosen, preferred_element_type=jnp.float32
        )

    products = lax.map(one_block, jnp.arange(tile_rows // 8, dtype=jnp.int32))
    partial_value = initial + products.reshape(initial.shape)
    own_rows = lax.psum_scatter(partial_value, "layer", scatter_dimension=0, tiled=True)
    return own_rows.astype(jnp.bfloat16)


def solution(mesh):
    return jax.shard_map(
        shards,
        mesh=mesh,
        in_specs=(
            P(("row", "col", "layer"), None, None, None),
            P(("row", "col", "layer")),
            P(("row", "col", "layer"), None),
        ),
        out_specs=P(("row", "layer"), "col", None, None),
        check_vma=False,
    )
```

profile of v0, /device:TPU:0, one launch (start us, length us, event | category | flops | bytes accessed | tf_op | source)
XLA Modules:
  0.0 2839.2 jit_solution(2040272807180117148)
XLA Ops:
  7.8 7.4 all-to-all-start
  15.2 14.1 copy.39
  29.3 6.1 all-to-all-start.4
  35.6 296.6 %all-to-all-done.4 = bf16[16,16,2,128,128]{4,3,2,0,1:T(8,128)(2,1)} async-done(((bf16[16,16,2,128,128]{4,3,2,0,1:T(8,128)(2,1)}), bf16[16,16,2,128,128]{4,3,2,0,1:T(8,128)(2,1)}, u32[]{:S(2)}, u32[]{:S(2)}) %all-to-all-start.4) | async-done | bytes 16777248 | tf_op jit(solution)/shard_map/all_to_all | solution.py:40
  332.1 5.5 broadcast_in_dim.81
  337.7 43.3 %scatter_fusion = bf16[128,2,128,128]{3,2,1,0:T(8,128)(2,1)} fusion(bf16[128,2,128,128]{3,2,1,0:T(8,128)(2,1)} %broadcast_in_dim.81, s32[256]{0:T(256)S(1)} %bitcast.92, bf16[256,2,128,128]{3,2,1,0:T(8,128)(2,1)} %bitcast.21), kind=kCustom, calls=%fused_computation.4 | custom fusion | bytes 50332672 | tf_op jit(solution)/shard_map/scatter | solution.py:56
  381.0 18.7 all_to_all.95
  399.7 10.4 copy.40
  411.6 69.9 %all-to-all-start.1 = ((s32[16,16,2]{0,2,1:T(2,128)}), s32[16,16,2]{0,2,1:T(2,128)S(1)}, u32[]{:S(2)}, u32[]{:S(2)}) async-start(s32[16,16,2]{0,2,1:T(2,128)} %bitcast.2), calls=%async_computation.1 | async-start | bytes 32768 | tf_op jit(solution)/shard_map/all_to_all | solution.py:41
  482.3 5.7 all-to-all-done.1
  493.5 16.8 all-gather
  522.7 152.2 %all-gather.5.cloned.1.call-done = bf16[128,4,128,128]{3,2,1,0:T(8,128)(2,1)} async-done(((bf16[64,4,128,128]{3,2,1,0:T(8,128)(2,1)}), bf16[128,4,128,128]{3,2,1,0:T(8,128)(2,1)}) %all-gather.5.cloned.1.call-update) | async-done | bytes 16777232 | tf_op jit(solution)/shard_map/all_gather | solution.py:68
  674.8 1268.5 %all-gather.7.cloned.1.call-done = bf16[128,16,128,128]{3,2,1,0:T(8,128)(2,1)} async-done(((bf16[128,2,128,128]{3,2,1,0:T(8,128)(2,1)}), bf16[128,16,128,128]{3,2,1,0:T(8,128)(2,1)}) %all-gather.7.cloned.1.call-update) | async-done | bytes 67108880 | tf_op jit(solution)/shard_map/all_gather | solution.py:76
  1943.3 834.9 %while.12 = (s32[]{:T(128)}, f32[16,8,4,128,128]{4,3,2,1,0:T(8,128)}, s32[16]{0:T(128)S(1)}, s32[128,16]{1,0:T(8,128)S(1)}, s32[16,8,4]{2,1,0:T(8,128)S(1)}, /*i...) while((s32[]{:T(128)}, ...), condition=%wide.region_4.5_spmd.clone, body=%wide.region_3.4_spmd.clone.sunk | while | flops 2155873536 | bytes 98579704 | solution.py:94
  1945.8 14.4 gather_fusion
  1960.3 21.6 copy.57
  1981.8 10.3 fusion.38
  1998.0 14.4 gather_fusion
  2012.4 21.6 copy.57
  2034.0 10.3 fusion.38
  2050.2 14.4 gather_fusion
  2064.7 21.6 copy.57
  2086.2 10.3 fusion.38
  2102.4 14.4 gather_fusion
  2116.8 21.6 copy.57
  2138.4 10.3 fusion.38
  2154.6 14.4 gather_fusion
  2169.0 21.6 copy.57
  2190.5 10.3 fusion.38
  2206.7 14.3 gather_fusion
  2221.1 21.6 copy.57
  2242.6 10.3 fusion.38
  2258.9 14.3 gather_fusion
  2273.2 21.6 copy.57
  2294.8 10.3 fusion.38
  2311.0 14.5 gather_fusion
  2325.5 21.6 copy.57
  2347.1 10.3 fusion.38
  2363.3 14.4 gather_fusion
  2377.7 21.6 copy.57
  2399.2 10.3 fusion.38
  2415.4 14.4 gather_fusion
  2429.9 21.6 copy.57
  2451.4 10.3 fusion.38
  2467.7 14.3 gather_fusion
  2482.0 21.6 copy.57
  2503.6 10.3 fusion.38
  2519.8 14.4 gather_fusion
  2534.2 21.6 copy.57
  2555.8 10.3 fusion.38
  2572.0 14.4 gather_fusion
  2586.4 21.6 copy.57
  2607.9 10.3 fusion.38
  2624.2 14.4 gather_fusion
  2638.6 21.6 copy.57
  2660.1 10.3 fusion.38
  2676.4 14.4 gather_fusion
  2690.8 21.6 copy.57
  2712.3 10.3 fusion.38
  2728.6 14.4 gather_fusion
  2743.0 21.6 copy.57
  2764.5 10.3 fusion.38
  2778.3 45.2 %reduce-scatter.2.cloned.1.call-done = f32[64,4,128,128]{3,2,1,0:T(8,128)} async-done(((f32[128,4,128,128]{3,2,1,0:T(8,128)}), f32[64,4,128,128]{3,2,1,0:T(8,128)}) %reduce-scatter.2.cloned.1.call-update) | async-done | bytes 16777232 | tf_op jit(solution)/shard_map/reduce_scatter | solution.py:96
  2823.5 9.2 convert_element_type.3
  (198 shorter events, 104.4 us)
Async XLA Ops:
  7.8 21.5 all-to-all-start
  29.3 302.8 %all-to-all-start.4 = ((bf16[16,16,2,128,128]{4,3,2,0,1:T(8,128)(2,1)}), bf16[16,16,2,128,128]{4,3,2,0,1:T(8,128)(2,1)}, u32[]{:S(2)}, u32[]{:S(2)}) async-start(bf16[16,16,2,128,128]{4,3,2,0,1:T(8,128)(2,1)} %copy.39), calls=%async_computation.4 | async-start | bytes 33554432 | tf_op jit(solution)/shard_map/all_to_all | solution.py:40
  35.4 639.5 %all-gather.5.cloned.1.call-start = ((), (), s32[]{:S(2)}) async-start(), calls=%async_computation.7 | async-start | bytes 25165824 | tf_op jit(solution)/shard_map/all_gather | solution.py:68
  399.7 11.2 copy-start
  410.2 1533.1 %all-gather.7.cloned.1.call-start = ((), (), s32[]{:S(2)}) async-start(), calls=%async_computation.8 | async-start | bytes 75497472 | tf_op jit(solution)/shard_map/all_gather | solution.py:76
  411.6 76.4 %all-to-all-start.1 = ((s32[16,16,2]{0,2,1:T(2,128)}), s32[16,16,2]{0,2,1:T(2,128)S(1)}, u32[]{:S(2)}, u32[]{:S(2)}) async-start(s32[16,16,2]{0,2,1:T(2,128)} %bitcast.2), calls=%async_computation.1 | async-start | bytes 32768 | tf_op jit(solution)/shard_map/all_to_all | solution.py:41
  490.2 20.1 all-to-all-start.2
  510.3 10.1 all-to-all-start.3
  513.7 2309.7 %reduce-scatter.2.cloned.1.call-start = ((), (), s32[]{:S(2)}) async-start(), calls=%async_computation.9 | async-start | bytes 50331648 | tf_op jit(solution)/shard_map/reduce_scatter | solution.py:96
Sparse Core Ops, SparseCore 0:
  410.3 264.4 all-gather.4
  676.4 1266.9 all-gather.6
  2778.4 45.0 reduce-scatter.1
where the time goes:
time: 2850 us; the launch traced here: 2840 us
  waiting for transfers between devices  1770 us (62%)
  local copies, waits for them, and re-layouts  738 us (26%)
  matrix products  165 us (6%)
  starting transfers between devices  90.2 us (3%)
  blocking collectives  39.9 us (1%)
    all_gather x1, waiting for transfers between devices, shards(): piece_blocks = lax.all_gather(row_tile, 'col', axis=1, tiled=True)  1270 us
    gather x32, local copies, waits for them, and re-layouts, one_block(): chosen = column_table[panel_steps[None, :], row_offsets]  575 us
    all_to_all x1, waiting for transfers between devices, shards(): lax.all_to_all(outgoing[0], ('col', 'layer'), split_axis=1, concat_axis=0...  297 us
    dot_general x16, matrix products, one_block(): jnp.einsum('mtab,mtsbc->msac', left_blocks, chosen, preferred_element_typ...  165 us
    all_gather x1, waiting for transfers between devices, shards(): lax.all_gather(column_tile, 'row', axis=0, tiled=True)  152 us
    all_to_all x1, starting transfers between devices, shards(): lax.all_to_all(outgoing[1], ('col', 'layer'), split_axis=1, concat_axis=0...  69.9 us
  transfers between devices with their start and end apart: 8, of which 6 were waited for; matrix products, arithmetic and copies ran while one was open for 1% of the time, Pallas kernels for 0%

commit v1 on v0

v1 whole, which is shorter than its diff:
```python
import functools

import jax
import jax.numpy as jnp
from jax import lax
from jax.experimental import pallas as pl
from jax.experimental.pallas import tpu as pltpu
from jax.sharding import PartitionSpec as P

MESH = pl.DeviceIdType.MESH
QUAD = 4


def pick_kernel(index_ref, got_ref, tile_ref, sems):
    count = tile_ref.shape[0]

    def copy(place):
        return pltpu.make_async_copy(
            got_ref.at[index_ref[place]], tile_ref.at[place], sems.at[place]
        )

    @pl.loop(0, count)
    def _(place):
        copy(place).start()

    @pl.loop(0, count)
    def _(place):
        copy(place).wait()


def pick_rows(index, got):
    count = index.shape[0]
    return pl.pallas_call(
        pick_kernel,
        out_shape=jax.ShapeDtypeStruct((count,) + got.shape[1:], got.dtype),
        in_specs=[
            pl.BlockSpec(memory_space=pltpu.SMEM),
            pl.BlockSpec(memory_space=pl.ANY),
        ],
        out_specs=pl.BlockSpec(memory_space=pl.ANY),
        scratch_shapes=[pltpu.SemaphoreType.DMA((count,))],
        name="pick_rows",
    )(index, got)


def spread_kernel(
    rows, cols, layers, outer, swapped, tile_ref, left_ref, right_ref,
    local_sem, send_sem, recv_sem, row_send, layer_send, table_recv,
):
    inner = cols // outer
    my_row, my_col, my_layer = (lax.axis_index(a) for a in ("row", "col", "layer"))
    my_outer, my_inner = my_col // inner, lax.rem(my_col, inner)
    my_group = my_row * layers + my_layer
    height = tile_ref.shape[0]

    barrier = pltpu.get_barrier_semaphore()
    lines = (
        (my_outer + 1 < outer, {"col": my_col + inner}),
        (my_outer >= 1, {"col": my_col - inner}),
        (my_inner + 1 < inner, {"col": my_col + 1}),
        (my_inner >= 1, {"col": my_col - 1}),
    )
    met = jnp.int32(rows - 1 + layers - 1)
    for there, device in lines:
        met = met + there.astype(jnp.int32)

        @pl.when(there)
        def _(device=device):
            pl.semaphore_signal(barrier, inc=1, device_id=device, device_id_type=MESH)

    row_peers = [lax.rem(my_row + d, rows) for d in range(1, rows)]
    layer_peers = [lax.rem(my_layer + d, layers) for d in range(1, layers)]
    for peer in row_peers:
        pl.semaphore_signal(barrier, inc=1, device_id={"row": peer}, device_id_type=MESH)
    for peer in layer_peers:
        pl.semaphore_signal(barrier, inc=1, device_id={"layer": peer}, device_id_type=MESH)
    pl.semaphore_wait(barrier, met)

    ending = []

    def send_left(kind, part, item, way, condition, own):
        def make():
            place = left_ref.at[item, part]
            return pltpu.make_async_remote_copy(
                src_ref=tile_ref.at[part] if own else place,
                dst_ref=place,
                send_sem=send_sem.at[kind, item, way],
                recv_sem=recv_sem.at[kind, item],
                device_id=lines[way][1],
                device_id_type=MESH,
            )

        condition = jnp.logical_and(condition, lines[way][0])

        @pl.when(condition)
        def _():
            make().start()

        ending.append((condition, make))

    def wait_left(kind, part, item, condition):
        @pl.when(condition)
        def _():
            place = left_ref.at[item, part]
            pltpu.make_async_remote_copy(
                src_ref=place,
                dst_ref=place,
                send_sem=send_sem.at[kind, item, 0],
                recv_sem=recv_sem.at[kind, item],
                device_id={"col": my_col},
                device_id_type=MESH,
            ).wait_recv()

    always = my_col >= 0
    axes = (
        (outer, inner, my_outer, (0, 1)),
        (inner, 1, my_inner, (2, 3)),
    )

    def stages(kind, part, first, second):
        size1, stride1, me1, ways1 = first
        size2, stride2, me2, ways2 = second

        def own():
            for way in ways1 + ways2:
                send_left(kind, part, my_col, way, always, True)

        def along_first(step):
            for sign, way in ((-1, ways1[0]), (1, ways1[1])):
                at = me1 + sign * step
                there = at >= 0 if sign < 0 else at < size1
                item = at * stride1 + me2 * stride2
                wait_left(kind, part, item, there)
                for onward in (way,) + ways2:
                    send_left(kind, part, item, onward, there, False)

        def along_second(step):
            for sign, way in ((-1, ways2[0]), (1, ways2[1])):
                at = me2 + sign * step
                there = at >= 0 if sign < 0 else at < size2
                for other in range(size1):
                    item = other * stride1 + at * stride2
                    wait_left(kind, part, item, there)
                    send_left(kind, part, item, way, there, False)

        return (
            [own]
            + [functools.partial(along_first, s) for s in range(1, size1)]
            + [functools.partial(along_second, s) for s in range(1, size2)]
        )

    main = stages(0, pl.ds(0, height - swapped), axes[0], axes[1])
    side = stages(1, pl.ds(height - swapped, swapped), axes[1], axes[0])

    def row_copy(d, peer):
        return pltpu.make_async_remote_copy(
            src_ref=tile_ref,
            dst_ref=right_ref.at[my_group],
            send_sem=row_send.at[d],
            recv_sem=table_recv.at[my_group],
            device_id={"row": peer},
            device_id_type=MESH,
        )

    def layer_copy(d, peer, row, own):
        group = row * layers + my_layer
        return pltpu.make_async_remote_copy(
            src_ref=tile_ref if own else right_ref.at[group],
            dst_ref=right_ref.at[group],
            send_sem=layer_send.at[d, row],
            recv_sem=table_recv.at[group],
            device_id={"layer": peer},
            device_id_type=MESH,
        )

    def wait_table(group):
        pltpu.make_async_remote_copy(
            src_ref=right_ref.at[group],
            dst_ref=right_ref.at[group],
            send_sem=row_send.at[0],
            recv_sem=table_recv.at[group],
            device_id={"row": my_row},
            device_id_type=MESH,
        ).wait_recv()

    side[0]()
    main[0]()
    for d, peer in enumerate(row_peers):
        row_copy(d, peer).start()
    for d, peer in enumerate(layer_peers):
        layer_copy(d, peer, my_row, True).start()
    locals_ = (
        pltpu.make_async_copy(tile_ref, left_ref.at[my_col], local_sem.at[0]),
        pltpu.make_async_copy(tile_ref, right_ref.at[my_group], local_sem.at[1]),
    )
    for copy in locals_:
        copy.start()
    side[1]()
    rest = side[2:]
    for index, stage in enumerate(main[1:]):
        stage()
        if index < len(rest):
            rest[index]()
        if index == 0:
            for peer in row_peers:
                wait_table(peer * layers + my_layer)
                for d, layer_peer in enumerate(layer_peers):
                    layer_copy(d, layer_peer, peer, False).start()
    for stage in rest[len(main) - 1:]:
        stage()
    for layer_peer in layer_peers:
        for row in range(rows):
            wait_table(row * layers + layer_peer)
    for copy in locals_:
        copy.wait()
    for condition, make in ending:

        @pl.when(condition)
        def _(make=make):
            make().wait_send()

    for d, peer in enumerate(row_peers):
        row_copy(d, peer).wait_send()
    for d, peer in enumerate(layer_peers):
        for row in [my_row] + row_peers:
            layer_copy(d, peer, row, True).wait_send()


def spread(tile, rows, cols, layers):
    outer = 4 if cols % 4 == 0 else 1
    swapped = max(tile.shape[0] // 8, 1)
    return pl.pallas_call(
        functools.partial(spread_kernel, rows, cols, layers, outer, swapped),
        out_shape=(
            jax.ShapeDtypeStruct((cols,) + tile.shape, tile.dtype),
            jax.ShapeDtypeStruct((rows * layers,) + tile.shape, tile.dtype),
        ),
        in_specs=[pl.BlockSpec(memory_space=pl.ANY)],
        out_specs=(pl.BlockSpec(memory_space=pl.ANY), pl.BlockSpec(memory_space=pl.ANY)),
        scratch_shapes=[
            pltpu.SemaphoreType.DMA((2,)),
            pltpu.SemaphoreType.DMA((2, cols, 4)),
            pltpu.SemaphoreType.DMA((2, cols)),
            pltpu.SemaphoreType.DMA((rows,)),
            pltpu.SemaphoreType.DMA((layers, rows)),
            pltpu.SemaphoreType.DMA((rows * layers,)),
        ],
        compiler_params=pltpu.CompilerParams(collective_id=0, has_side_effects=True),
        name="spread",
    )(tile)


def multiply_kernel(pair_ref, turns_ref, left_ref, right_hbm, out_ref, table, sem):
    row = pl.program_id(0)
    nb = right_hbm.shape[0]
    width = out_ref.shape[1]
    panels = left_ref.shape[0] * left_ref.shape[2]

    @pl.when(row == 0)
    def _():
        copy = pltpu.make_async_copy(right_hbm, table.at[pl.ds(0, nb)], sem)
        copy.start()
        table[nb] = jnp.zeros_like(table[nb])
        copy.wait()

    group = 2 if width % 2 == 0 else 1
    for base in range(0, width, group):

        def step(turn, sums, base=base):
            new = []
            for j in range(group):
                start = (row * width + base + j) * panels + turn * QUAD
                lefts, rights = [], []
                for q in range(QUAD):
                    code = pair_ref[start + q]
                    panel, place = code // 1024, lax.rem(code, 1024)
                    lefts.append(left_ref[panel // width, 0, lax.rem(panel, width)])
                    rights.append(table[place, base + j])
                new.append(
                    sums[j]
                    + jnp.dot(
                        jnp.concatenate(lefts, axis=1),
                        jnp.concatenate(rights, axis=0),
                        preferred_element_type=jnp.float32,
                    )
                )
            return tuple(new)

        zero = jnp.zeros(out_ref.shape[2:], jnp.float32)
        turns = turns_ref[row * width + base]
        for j in range(1, group):
            turns = jnp.maximum(turns, turns_ref[row * width + base + j])
        sums = lax.fori_loop(0, turns, step, (zero,) * group)
        for j in range(group):
            out_ref[0, base + j] = sums[j].astype(out_ref.dtype)


def multiply(pairs, turns, left, right):
    cols, height, width, size, _ = left.shape
    nb = right.shape[0]
    table_bytes = (nb + 1) * width * size * size * 2
    return pl.pallas_call(
        multiply_kernel,
        out_shape=jax.ShapeDtypeStruct((height, width, size, size), left.dtype),
        grid_spec=pltpu.PrefetchScalarGridSpec(
            num_scalar_prefetch=2,
            grid=(height,),
            in_specs=[
                pl.BlockSpec((cols, 1, width, size, size), lambda i, *_: (0, i, 0, 0, 0)),
                pl.BlockSpec(memory_space=pl.ANY),
            ],
            out_specs=pl.BlockSpec((1, width, size, size), lambda i, *_: (i, 0, 0, 0)),
            scratch_shapes=[
                pltpu.VMEM((nb + 1, width, size, size), left.dtype),
                pltpu.SemaphoreType.DMA,
            ],
        ),
        compiler_params=pltpu.CompilerParams(vmem_limit_bytes=table_bytes + (10 << 20)),
        name="multiply",
    )(pairs, turns, left, right)


def shards(owned_blocks, slot_rows, block_cols):
    own_slots, panels, size, _ = owned_blocks.shape
    rows = lax.axis_size("row")
    cols = lax.axis_size("col")
    layers = lax.axis_size("layer")
    width = panels // cols
    slots = own_slots * rows * cols * layers
    my_row, my_col, my_layer = (lax.axis_index(a) for a in ("row", "col", "layer"))
    my_group = my_row * layers + my_layer

    got = lax.all_to_all(
        owned_blocks.reshape(own_slots, cols, width, size, size),
        "col", split_axis=1, concat_axis=0, tiled=True,
    ).reshape(cols * own_slots, width, size, size)

    ids = jnp.concatenate([slot_rows[:, None], block_cols], axis=1)
    ids = lax.all_gather(ids, ("row", "col", "layer"), axis=0, tiled=True)
    nb = NB
    per_layer = panels // (cols * layers) * (nb // panels)
    height = nb // (rows * layers)
    place = jnp.arange(nb, dtype=jnp.int32)
    part, within = place // height, place % height
    row_at = (
        part // layers * (nb // rows)
        + within // per_layer * per_layer * layers
        + part % layers * per_layer
        + within % per_layer
    )
    holds = ids[None, :, 0] == row_at[:, None]
    slot_at = jnp.sum(
        jnp.where(holds, jnp.arange(slots, dtype=jnp.int32)[None, :], 0), axis=1
    )
    my_slots = lax.dynamic_slice_in_dim(slot_at, my_group * height, height)
    owner = my_slots // own_slots // layers % cols
    tile = pick_rows(owner * own_slots + my_slots % own_slots, got)
    left, right = spread(tile, rows, cols, layers)

    columns = ids[slot_at, 1:]
    place_of = jnp.sum(
        jnp.where(row_at[:, None] == place[None, :], place[:, None], 0), axis=0
    )
    mine = lax.dynamic_slice_in_dim(columns, my_group * height, height)
    wanted = lax.dynamic_slice_in_dim(mine, my_col * width, width, 1)
    partner = place_of[mine]
    reach = lax.dynamic_slice_in_dim(columns, my_col * width, width, 1)
    matched = reach[partner] == wanted[:, None, :]
    matched = matched.transpose(0, 2, 1)
    order = jnp.cumsum(matched.astype(jnp.int32), axis=2) - 1
    code = jnp.arange(panels, dtype=jnp.int32)[None, :] * 1024 + partner
    lane = jnp.arange(panels, dtype=jnp.int32)
    taken = matched[..., None] & (order[..., None] == lane)
    pairs = jnp.sum(jnp.where(taken, (code - nb)[:, None, :, None], 0), axis=2) + nb
    turns = (jnp.sum(matched, axis=2, dtype=jnp.int32) + QUAD - 1) // QUAD
    return multiply(
        pairs.reshape(-1), turns.reshape(-1), left, right.reshape(nb, width, size, size)
    )


NB = 256


def solution(mesh):
    return jax.shard_map(
        shards,
        mesh=mesh,
        in_specs=(
            P(("row", "col", "layer"), None, None, None),
            P(("row", "col", "layer")),
            P(("row", "col", "layer"), None),
        ),
        out_specs=P(("row", "layer"), "col", None, None),
        check_vma=False,
    )
```

time: 2850 us -> 2070 us (0.73)
  waiting for transfers between devices: 1770 us -> 0.01 us
  Pallas kernels: 0 us -> 1100 us
  blocking collectives: 39.9 us -> 390 us
  local copies, waits for them, and re-layouts: 738 us -> 557 us
  matrix products: 165 us -> 0 us
  starting transfers between devices: 90.2 us -> 7.41 us
    all_gather x2 -> x0, waiting for transfers between devices: 1420 us -> none  [the longest x1 1270 us: shards(): piece_blocks = lax.all_gather(row_tile, 'col', axis=1, tiled=True)]
    pallas_call x0 -> x3, Pallas kernels: none -> 1100 us  [the longest x1 724 us: spread(): pl.pallas_call(functools.partial(spread_kernel, rows, cols, layers, outer...]
    all_gather x2 -> x1, blocking collectives: 21.1 us -> 390 us  [shards(): ids = lax.all_gather(ids, ('row', 'col', 'layer'), axis=0, tiled=True)]
    all_to_all x5 -> x1, waiting for transfers between devices: 303 us -> 0.01 us  [shards(): lax.all_to_all(owned_blocks.reshape(own_slots, cols, width, size, size),...]
    dot_general x16 -> x0, matrix products: 165 us -> none  [one_block(): jnp.einsum('mtab,mtsbc->msac', left_blocks, chosen, preferred_element_typ...]
    all_to_all x5 -> x1, starting transfers between devices: 90.1 us -> 7.41 us  [shards(): lax.all_to_all(owned_blocks.reshape(own_slots, cols, width, size, size),...]
    dynamic_update_slice x32 -> x0, local copies, waits for them, and re-layouts: 54.4 us -> none  [shards(): products = lax.map(one_block, jnp.arange(tile_rows // 8, dtype=jnp.int32))]
    gather x48 -> x1029, local copies, waits for them, and re-layouts: 591 us -> 542 us  [the longest x32 575 us: one_block(): chosen = column_table[panel_steps[None, :], row_offsets]]
  transfers between devices with their start and end apart: 8 -> 1, of which waited for: 6 -> 0; matrix products, arithmetic and copies ran while one was open for 1% -> 27% of each run, Pallas kernels for 0% -> 0%
where the time goes in v1:
time: 2070 us; the launch traced here: 2060 us
  Pallas kernels  1100 us (53%)
  local copies, waits for them, and re-layouts  557 us (27%)
  blocking collectives  390 us (19%)
    pallas_call x1, Pallas kernels, spread(): pl.pallas_call(functools.partial(spread_kernel, rows, cols, layers, outer...  724 us
    gather x1024, local copies, waits for them, and re-layouts  522 us
    all_gather x1, blocking collectives, shards(): ids = lax.all_gather(ids, ('row', 'col', 'layer'), axis=0, tiled=True)  390 us
    pallas_call x1, Pallas kernels, pick_rows(): pl.pallas_call(pick_kernel, out_shape=jax.ShapeDtypeStruct((count,) + got...  256 us
    pallas_call x1, Pallas kernels, multiply(): pl.pallas_call(multiply_kernel, out_shape=jax.ShapeDtypeStruct((height, w...  120 us
  transfers between devices with their start and end apart: 1, of which 0 were waited for; matrix products, arithmetic and copies ran while one was open for 27% of the time, Pallas kernels for 0%

profile of v1, /device:TPU:0, one launch (start us, length us, event | category | flops | bytes accessed | tf_op | source)
XLA Modules:
  0.0 2059.1 jit_solution(8491129162188644278)
XLA Ops:
  0.0 14.1 copy.31
  14.1 7.4 all-to-all-start
  21.7 390.0 %all_gather.3 = s32[512,33]{1,0:T(8,128)S(1)} all-gather(s32[16,33]{1,0:T(8,128)S(1)} %pad_add_fusion), channel_id=1, replica_groups=mesh['row'=2,'col'=8,'layer'=2] {'row','col','layer'}, dimensions={0}, use_global_device_ids=true | all-gather | bytes 69696 | tf_op jit(solution)/shard_map/all_gather | solution.py:339
  412.1 523.5 %while.1 = (s32[]{:T(128)}, s32[512,33]{1,0:T(8,128)S(1)}, s32[256,2]{0,1:T(2,128)S(1)}, s32[256,32]{1,0:T(8,128)S(1)}, s32[]{:T(128)}, /*index=5*/s32[]{:T(128)}) while((s32[]{:T(128)}, s32[512,33]{1,0:T(8,128)S(1)}, s32[256,2]{0,1:T(2,128)S(1)}, s32[256,32]{1,0:T(8,128)S(1)}, s32[]{:T(128)}, /*index=5*/s32[]{:T(128)}) %tuple.20), condition=%wide.while_cond, body=%wide.while_body.sunk | while | flops 2 | bytes 633 | solution.py:360
  412.7 1.4 dynamic-slice.7
  414.8 1.4 dynamic-slice.7
  418.9 1.4 dynamic-slice.7
  420.9 1.4 dynamic-slice.7
  423.0 1.4 dynamic-slice.7
  425.0 1.4 dynamic-slice.7
  427.1 1.4 dynamic-slice.7
  431.1 1.4 dynamic-slice.7
  433.2 1.4 dynamic-slice.7
  435.2 1.4 dynamic-slice.7
  437.3 1.4 dynamic-slice.7
  439.3 1.4 dynamic-slice.7
  441.4 1.4 dynamic-slice.7
  443.4 1.4 dynamic-slice.7
  445.5 1.4 dynamic-slice.7
  447.5 1.4 dynamic-slice.7
  449.5 1.4 dynamic-slice.7
  451.6 1.4 dynamic-slice.7
  453.6 1.4 dynamic-slice.7
  457.7 1.4 dynamic-slice.7
  459.8 1.4 dynamic-slice.7
  461.8 1.4 dynamic-slice.7
  463.9 1.4 dynamic-slice.7
  465.9 1.4 dynamic-slice.7
  470.0 1.4 dynamic-slice.7
  472.0 1.4 dynamic-slice.7
  474.1 1.4 dynamic-slice.7
  476.1 1.4 dynamic-slice.7
  478.2 1.4 dynamic-slice.7
  480.2 1.4 dynamic-slice.7
  482.3 1.4 dynamic-slice.7
  484.3 1.4 dynamic-slice.7
  486.3 1.4 dynamic-slice.7
  488.4 1.4 dynamic-slice.7
  490.4 1.4 dynamic-slice.7
  492.5 1.4 dynamic-slice.7
  496.6 1.4 dynamic-slice.7
  498.6 1.4 dynamic-slice.7
  500.7 1.4 dynamic-slice.7
  502.7 1.4 dynamic-slice.7
  504.8 1.4 dynamic-slice.7
  508.8 1.4 dynamic-slice.7
  510.9 1.4 dynamic-slice.7
  512.9 1.4 dynamic-slice.7
  515.0 1.4 dynamic-slice.7
  517.0 1.4 dynamic-slice.7
  519.1 1.4 dynamic-slice.7
  521.1 1.4 dynamic-slice.7
  523.2 1.4 dynamic-slice.7
  525.2 1.4 dynamic-slice.7
  527.2 1.4 dynamic-slice.7
  529.3 1.4 dynamic-slice.7
  531.3 1.4 dynamic-slice.7
  535.4 1.4 dynamic-slice.7
  537.5 1.4 dynamic-slice.7
  935.8 13.1 gather_fusion
  949.4 5.5 gather_fusion.1
  958.6 256.5 %pick_rows.1.tile_ref = bf16[64,4,128,128]{3,2,1,0:T(8,128)(2,1)} custom-call(s32[64]{0:T(128)} %fusion.6.index_ref, bf16[128,4,128,128]{3,2,1,0:T(8,128)(2,1)} %bitcast.7.got_ref), custom_call_target="tpu_custom_call" | custom-call | tf_op jit(solution)/shard_map/pick_rows/pallas_call | solution.py:33
  1215.0 723.7 %spread.1 = (bf16[8,64,4,128,128]{4,3,2,1,0:T(8,128)(2,1)}, bf16[4,64,4,128,128]{4,3,2,1,0:T(8,128)(2,1)}) custom-call(bf16[64,4,128,128]{3,2,1,0:T(8,128)(2,1)} %pick_rows.1.tile_ref), custom_call_target="tpu_custom_call" | custom-call | tf_op jit(solution)/shard_map/spread/pallas_call | solution.py:232
  1938.7 120.4 %multiply.3 = bf16[64,4,128,128]{3,2,1,0:T(8,128)(2,1)} custom-call(s32[8192]{0:T(1024)S(1)} %add.189.pair_ref, s32[256]{0:T(256)S(1)} %and_select_fusion.4.turns_ref, bf16[8,64,4,128,128]{4,3,2,1,0:T(8,128)(2,1)} %get-tuple-element.7.left_ref, bf16[256,4,128,128]{3,2,1,0:T(8,128)(2,1)} %bitcast.21), custom_call_target="tpu_custom_call" | custom-call | tf_op jit(solution)/shard_map/multiply/pallas_call | solution.py:302
  (1013 shorter events, 452.7 us)
Async XLA Ops:
  14.1 7.4 copy-start.1
  14.1 7.5 copy-start
  14.1 944.5 %all-to-all-start = ((bf16[16,8,4,128,128]{4,3,2,0,1:T(8,128)(2,1)}), bf16[16,8,4,128,128]{4,3,2,0,1:T(8,128)(2,1)}, u32[]{:S(2)}, u32[]{:S(2)}) async-start(bf16[16,8,4,128,128]{4,3,2,0,1:T(8,128)(2,1)} %copy.31), calls=%async_computation | async-start | bytes 33554432 | tf_op jit(solution)/shard_map/all_to_all | solution.py:333

commit v2 on v1

--- a/solution.py
+++ b/solution.py
@@ -11,47 +11,44 @@
 QUAD = 4
 
 
-def pick_kernel(index_ref, got_ref, tile_ref, sems):
-    count = tile_ref.shape[0]
-
-    def copy(place):
-        return pltpu.make_async_copy(
-            got_ref.at[index_ref[place]], tile_ref.at[place], sems.at[place]
-        )
-
-    @pl.loop(0, count)
-    def _(place):
-        copy(place).start()
-
-    @pl.loop(0, count)
-    def _(place):
-        copy(place).wait()
-
-
-def pick_rows(index, got):
-    count = index.shape[0]
+def pick_kernel(index_ref, spot_ref, got_ref, left_ref, right_ref):
+    block = got_ref[0]
+    left_ref[0, 0] = block
+    right_ref[0, 0] = block
+
+
+def pick_rows(index, spot, got, cols, groups):
+    height = index.shape[0]
+    block = got.shape[1:]
     return pl.pallas_call(
         pick_kernel,
-        out_shape=jax.ShapeDtypeStruct((count,) + got.shape[1:], got.dtype),
-        in_specs=[
-            pl.BlockSpec(memory_space=pltpu.SMEM),
-            pl.BlockSpec(memory_space=pl.ANY),
-        ],
-        out_specs=pl.BlockSpec(memory_space=pl.ANY),
-        scratch_shapes=[pltpu.SemaphoreType.DMA((count,))],
+        out_shape=(
+            jax.ShapeDtypeStruct((cols, height) + block, got.dtype),
+            jax.ShapeDtypeStruct((groups, height) + block, got.dtype),
+        ),
+        grid_spec=pltpu.PrefetchScalarGridSpec(
+            num_scalar_prefetch=2,
+            grid=(height,),
+            in_specs=[
+                pl.BlockSpec((1,) + block, lambda i, index, spot: (index[i], 0, 0, 0)),
+            ],
+            out_specs=(
+                pl.BlockSpec((1, 1) + block, lambda i, index, spot: (spot[0], i, 0, 0, 0)),
+                pl.BlockSpec((1, 1) + block, lambda i, index, spot: (spot[1], i, 0, 0, 0)),
+            ),
+        ),
         name="pick_rows",
-    )(index, got)
+    )(index, spot, got)
 
 
 def spread_kernel(
-    rows, cols, layers, outer, swapped, tile_ref, left_ref, right_ref,
-    local_sem, send_sem, recv_sem, row_send, layer_send, table_recv,
+    rows, cols, layers, outer, parts, left_in, right_in, left_ref, right_ref,
+    send_sem, recv_sem, row_send, layer_send, table_recv,
 ):
     inner = cols // outer
     my_row, my_col, my_layer = (lax.axis_index(a) for a in ("row", "col", "layer"))
     my_outer, my_inner = my_col // inner, lax.rem(my_col, inner)
     my_group = my_row * layers + my_layer
-    height = tile_ref.shape[0]
 
     barrier = pltpu.get_barrier_semaphore()
     lines = (
@@ -78,11 +75,11 @@
 
     ending = []
 
-    def send_left(kind, part, item, way, condition, own):
+    def send_left(kind, part, item, way, condition):
         def make():
             place = left_ref.at[item, part]
             return pltpu.make_async_remote_copy(
-                src_ref=tile_ref.at[part] if own else place,
+                src_ref=place,
                 dst_ref=place,
                 send_sem=send_sem.at[kind, item, way],
                 recv_sem=recv_sem.at[kind, item],
@@ -123,7 +120,7 @@
 
         def own():
             for way in ways1 + ways2:
-                send_left(kind, part, my_col, way, always, True)
+                send_left(kind, part, my_col, way, always)
 
         def along_first(step):
             for sign, way in ((-1, ways1[0]), (1, ways1[1])):
@@ -132,7 +129,7 @@
                 item = at * stride1 + me2 * stride2
                 wait_left(kind, part, item, there)
                 for onward in (way,) + ways2:
-                    send_left(kind, part, item, onward, there, False)
+                    send_left(kind, part, item, onward, there)
 
         def along_second(step):
             for sign, way in ((-1, ways2[0]), (1, ways2[1])):
@@ -141,7 +138,7 @@
                 for other in range(size1):
                     item = other * stride1 + at * stride2
                     wait_left(kind, part, item, there)
-                    send_left(kind, part, item, way, there, False)
+                    send_left(kind, part, item, way, there)
 
         return (
             [own]
@@ -149,12 +146,14 @@
             + [functools.partial(along_second, s) for s in range(1, size2)]
         )
 
-    main = stages(0, pl.ds(0, height - swapped), axes[0], axes[1])
-    side = stages(1, pl.ds(height - swapped, swapped), axes[1], axes[0])
+    plans = [
+        stages(kind, pl.ds(start, size), *(axes if straight else axes[::-1]))
+        for kind, (start, size, straight) in enumerate(parts)
+    ]
 
     def row_copy(d, peer):
         return pltpu.make_async_remote_copy(
-            src_ref=tile_ref,
+            src_ref=right_ref.at[my_group],
             dst_ref=right_ref.at[my_group],
             send_sem=row_send.at[d],
             recv_sem=table_recv.at[my_group],
@@ -162,10 +161,10 @@
             device_id_type=MESH,
         )
 
-    def layer_copy(d, peer, row, own):
+    def layer_copy(d, peer, row):
         group = row * layers + my_layer
         return pltpu.make_async_remote_copy(
-            src_ref=tile_ref if own else right_ref.at[group],
+            src_ref=right_ref.at[group],
             dst_ref=right_ref.at[group],
             send_sem=layer_send.at[d, row],
             recv_sem=table_recv.at[group],
@@ -183,36 +182,23 @@
             device_id_type=MESH,
         ).wait_recv()
 
-    side[0]()
-    main[0]()
+    for plan in plans:
+        plan[0]()
     for d, peer in enumerate(row_peers):
         row_copy(d, peer).start()
     for d, peer in enumerate(layer_peers):
-        layer_copy(d, peer, my_row, True).start()
-    locals_ = (
-        pltpu.make_async_copy(tile_ref, left_ref.at[my_col], local_sem.at[0]),
-        pltpu.make_async_copy(tile_ref, right_ref.at[my_group], local_sem.at[1]),
-    )
-    for copy in locals_:
-        copy.start()
-    side[1]()
-    rest = side[2:]
-    for index, stage in enumerate(main[1:]):
-        stage()
-        if index < len(rest):
-            rest[index]()
-        if index == 0:
+        layer_copy(d, peer, my_row).start()
+    for index in range(1, len(plans[0])):
+        for plan in plans:
+            plan[index]()
+        if index == 1:
             for peer in row_peers:
                 wait_table(peer * layers + my_layer)
                 for d, layer_peer in enumerate(layer_peers):
-                    layer_copy(d, layer_peer, peer, False).start()
-    for stage in rest[len(main) - 1:]:
-        stage()
+                    layer_copy(d, layer_peer, peer).start()
     for layer_peer in layer_peers:
         for row in range(rows):
             wait_table(row * layers + layer_peer)
-    for copy in locals_:
-        copy.wait()
     for condition, make in ending:
 
         @pl.when(condition)
@@ -223,31 +209,37 @@
         row_copy(d, peer).wait_send()
     for d, peer in enumerate(layer_peers):
         for row in [my_row] + row_peers:
-            layer_copy(d, peer, row, True).wait_send()
-
-
-def spread(tile, rows, cols, layers):
+            layer_copy(d, peer, row).wait_send()
+
+
+def spread(left, right, rows, cols, layers):
     outer = 4 if cols % 4 == 0 else 1
-    swapped = max(tile.shape[0] // 8, 1)
+    height = left.shape[1]
+    swapped = max(height // 8, 1)
+    count = min(4, height - swapped)
+    cuts = [swapped + (height - swapped) * k // count for k in range(count + 1)]
+    parts = [(0, swapped, False)]
+    parts += [(lo, hi - lo, True) for lo, hi in zip(cuts, cuts[1:])]
+    kinds = len(parts)
     return pl.pallas_call(
-        functools.partial(spread_kernel, rows, cols, layers, outer, swapped),
+        functools.partial(spread_kernel, rows, cols, layers, outer, tuple(parts)),
         out_shape=(
-            jax.ShapeDtypeStruct((cols,) + tile.shape, tile.dtype),
-            jax.ShapeDtypeStruct((rows * layers,) + tile.shape, tile.dtype),
-        ),
-        in_specs=[pl.BlockSpec(memory_space=pl.ANY)],
+            jax.ShapeDtypeStruct(left.shape, left.dtype),
+            jax.ShapeDtypeStruct(right.shape, right.dtype),
+        ),
+        in_specs=[pl.BlockSpec(memory_space=pl.ANY), pl.BlockSpec(memory_space=pl.ANY)],
         out_specs=(pl.BlockSpec(memory_space=pl.ANY), pl.BlockSpec(memory_space=pl.ANY)),
+        input_output_aliases={0: 0, 1: 1},
         scratch_shapes=[
-            pltpu.SemaphoreType.DMA((2,)),
-            pltpu.SemaphoreType.DMA((2, cols, 4)),
-            pltpu.SemaphoreType.DMA((2, cols)),
+            pltpu.SemaphoreType.DMA((kinds, cols, 4)),
+            pltpu.SemaphoreType.DMA((kinds, cols)),
             pltpu.SemaphoreType.DMA((rows,)),
             pltpu.SemaphoreType.DMA((layers, rows)),
             pltpu.SemaphoreType.DMA((rows * layers,)),
         ],
         compiler_params=pltpu.CompilerParams(collective_id=0, has_side_effects=True),
         name="spread",
-    )(tile)
+    )(left, right)
 
 
 def multiply_kernel(pair_ref, turns_ref, left_ref, right_hbm, out_ref, table, sem):
@@ -330,13 +322,14 @@
     my_row, my_col, my_layer = (lax.axis_index(a) for a in ("row", "col", "layer"))
     my_group = my_row * layers + my_layer
 
+    ids = jnp.concatenate([slot_rows[:, None], block_cols], axis=1)
+    ids = lax.all_gather(ids, ("row", "col", "layer"), axis=0, tiled=True)
+    owned_blocks, ids = lax.optimization_barrier((owned_blocks, ids))
     got = lax.all_to_all(
         owned_blocks.reshape(own_slots, cols, width, size, size),
         "col", split_axis=1, concat_axis=0, tiled=True,
     ).reshape(cols * own_slots, width, size, size)
 
-    ids = jnp.concatenate([slot_rows[:, None], block_cols], axis=1)
-    ids = lax.all_gather(ids, ("row", "col", "layer"), axis=0, tiled=True)
     nb = NB
     per_layer = panels // (cols * layers) * (nb // panels)
     height = nb // (rows * layers)
@@ -354,16 +347,26 @@
     )
     my_slots = lax.dynamic_slice_in_dim(slot_at, my_group * height, height)
     owner = my_slots // own_slots // layers % cols
-    tile = pick_rows(owner * own_slots + my_slots % own_slots, got)
-    left, right = spread(tile, rows, cols, layers)
-
-    columns = ids[slot_at, 1:]
-    place_of = jnp.sum(
-        jnp.where(row_at[:, None] == place[None, :], place[:, None], 0), axis=0
-    )
+    left, right = pick_rows(
+        owner * own_slots + my_slots % own_slots,
+        jnp.stack([my_col, my_group]).astype(jnp.int32),
+        got, cols, rows * layers,
+    )
+    left, right = spread(left, right, rows, cols, layers)
+
+    columns = jnp.dot(
+        holds.astype(jnp.float32),
+        ids[:, 1:].astype(jnp.float32),
+        precision=lax.Precision.HIGHEST,
+    ).astype(jnp.int32)
     mine = lax.dynamic_slice_in_dim(columns, my_group * height, height)
     wanted = lax.dynamic_slice_in_dim(mine, my_col * width, width, 1)
-    partner = place_of[mine]
+    inside = mine % (nb // rows)
+    partner = (
+        (mine // (nb // rows) * layers + inside // per_layer % layers) * height
+        + inside // (per_layer * layers) * per_layer
+        + inside % per_layer
+    )
     reach = lax.dynamic_slice_in_dim(columns, my_col * width, width, 1)
     matched = reach[partner] == wanted[:, None, :]
     matched = matched.transpose(0, 2, 1)

time: 2070 us -> 1250 us (0.60)
  local copies, waits for them, and re-layouts: 557 us -> 22 us
  waiting for transfers between devices: 0.01 us -> 352 us
  blocking collectives: 390 us -> 43.9 us
  Pallas kernels: 1100 us -> 815 us
    gather x1027 -> x0, local copies, waits for them, and re-layouts: 536 us -> none
    all_to_all x1, waiting for transfers between devices: 0.01 us -> 352 us  [shards(): lax.all_to_all(owned_blocks.reshape(own_slots, cols, width, size, size),...]
    all_gather x1, blocking collectives: 390 us -> 43.9 us  [shards(): ids = lax.all_gather(ids, ('row', 'col', 'layer'), axis=0, tiled=True)]
    pallas_call x1, Pallas kernels: 256 us -> 36.8 us  [pick_rows(): pl.pallas_call(pick_kernel, out_shape=(jax.ShapeDtypeStruct((cols, height...]
    pallas_call x1, Pallas kernels: 724 us -> 657 us  [spread(): pl.pallas_call(functools.partial(spread_kernel, rows, cols, layers, outer...]
  transfers between devices with their start and end apart: 1 -> 1, of which waited for: 0 -> 1; matrix products, arithmetic and copies ran while one was open for 27% -> 1% of each run, Pallas kernels for 0% -> 0%
where the time goes in v2:
time: 1250 us; the launch traced here: 1240 us
  Pallas kernels  815 us (65%)
  waiting for transfers between devices  352 us (28%)
  blocking collectives  43.9 us (4%)
  local copies, waits for them, and re-layouts  22 us (2%)
    pallas_call x1, Pallas kernels, spread(): pl.pallas_call(functools.partial(spread_kernel, rows, cols, layers, outer...  657 us
    all_to_all x1, waiting for transfers between devices, shards(): lax.all_to_all(owned_blocks.reshape(own_slots, cols, width, size, size),...  352 us
    pallas_call x1, Pallas kernels, multiply(): pl.pallas_call(multiply_kernel, out_shape=jax.ShapeDtypeStruct((height, w...  121 us
    all_gather x1, blocking collectives, shards(): ids = lax.all_gather(ids, ('row', 'col', 'layer'), axis=0, tiled=True)  43.9 us
    pallas_call x1, Pallas kernels, pick_rows(): pl.pallas_call(pick_kernel, out_shape=(jax.ShapeDtypeStruct((cols, height...  36.8 us
  transfers between devices with their start and end apart: 1, of which 1 were waited for; matrix products, arithmetic and copies ran while one was open for 1% of the time, Pallas kernels for 0%

profile of v2, /device:TPU:0, one launch (start us, length us, event | category | flops | bytes accessed | tf_op | source)
XLA Modules:
  0.0 1244.2 jit_solution(4112073729884296442)
XLA Ops:
  0.0 0.7 copy.30
  0.7 0.8 pad_add_fusion
  1.5 43.9 %all_gather.3 = s32[512,33]{1,0:T(8,128)S(1)} all-gather(s32[16,33]{1,0:T(8,128)S(1)} %pad_add_fusion), channel_id=1, replica_groups=mesh['row'=2,'col'=8,'layer'=2] {'row','col','layer'}, dimensions={0}, use_global_device_ids=true | all-gather | bytes 69696 | tf_op jit(solution)/shard_map/all_gather | solution.py:326
  45.4 14.1 %copy.38 = bf16[16,8,4,128,128]{4,3,2,0,1:T(8,128)(2,1)} copy(bf16[16,8,4,128,128]{4,3,2,1,0:T(8,128)(2,1)} %bitcast.15) | data formatting | bytes 33554432 | tf_op jit(solution)/shard_map/reshape | solution.py:329
  59.5 5.7 all-to-all-start
  65.3 0.1 slice_reduce_fusion
  65.4 0.5 convolution_convert_fusion
  65.9 0.1 compare_select_fusion.1
  66.0 0.1 copy.31
  66.1 0.1 reshape.117
  66.2 0.1 copy.32
  66.4 5.5 gather_fusion
  71.8 0.5 copy.33
  72.4 0.1 dynamic_slice.14
  72.5 0.2 convert_reduce_fusion
  72.7 0.1 copy.34
  72.8 0.1 copy.37
  72.9 0.1 sub.71
  73.0 0.8 reduce_window_sum.11
  73.9 0.1 copy.35
  74.0 0.1 add_add_fusion
  74.0 0.6 select_reduce_fusion
  74.7 0.1 copy.36
  74.8 0.1 add.173.pair_ref
  74.9 0.2 fusion.2
  75.1 0.7 fusion.26.index_ref
  75.8 0.7 pad_add_fusion.1.spot_ref
  76.5 352.4 %all-to-all-done = bf16[16,8,4,128,128]{4,3,2,0,1:T(8,128)(2,1)} async-done(((bf16[16,8,4,128,128]{4,3,2,0,1:T(8,128)(2,1)}), bf16[16,8,4,128,128]{4,3,2,0,1:T(8,128)(2,1)}, u32[]{:S(2)}, u32[]{:S(2)}) %all-to-all-start) | async-done | bytes 16777248 | tf_op jit(solution)/shard_map/all_to_all | solution.py:328
  428.9 36.8 %pick_rows.1 = (bf16[8,64,4,128,128]{4,3,2,1,0:T(8,128)(2,1)}, bf16[4,64,4,128,128]{4,3,2,1,0:T(8,128)(2,1)}) custom-call(s32[64]{0:T(128)} %fusion.26.index_ref, s32[2]{0:T(128)} %pad_add_fusion.1.spot_ref, bf16[128,4,128,128]{3,2,1,0:T(8,128)(2,1)} %bitcast.8.got_ref), custom_call_target="tpu_custom_call" | custom-call | tf_op jit(solution)/shard_map/pick_rows/pallas_call | solution.py:23
  465.6 657.3 %spread.1 = (bf16[8,64,4,128,128]{4,3,2,1,0:T(8,128)(2,1)}, bf16[4,64,4,128,128]{4,3,2,1,0:T(8,128)(2,1)}) custom-call(bf16[8,64,4,128,128]{4,3,2,1,0:T(8,128)(2,1)} %get-tuple-element.13.left_in, bf16[4,64,4,128,128]{4,3,2,1,0:T(8,128)(2,1)} %get-tuple-element.14.right_in), custom_call_target="tpu_custom_call", output_to_operand_aliasing={{0}: (0, {}), {1}: (1, {})} | custom-call | tf_op jit(solution)/shard_map/spread/pallas_call | solution.py:224
  1123.0 121.2 %multiply.3 = bf16[64,4,128,128]{3,2,1,0:T(8,128)(2,1)} custom-call(s32[8192]{0:T(1024)S(1)} %add.173.pair_ref, s32[256]{0:T(256)S(1)} %and_select_fusion.4.turns_ref, bf16[8,64,4,128,128]{4,3,2,1,0:T(8,128)(2,1)} %get-tuple-element.15.left_ref, bf16[256,4,128,128]{3,2,1,0:T(8,128)(2,1)} %bitcast.14), custom_call_target="tpu_custom_call" | custom-call | tf_op jit(solution)/shard_map/multiply/pallas_call | solution.py:294
  (9 shorter events, 0.1 us)
Async XLA Ops:
  59.5 369.3 %all-to-all-start = ((bf16[16,8,4,128,128]{4,3,2,0,1:T(8,128)(2,1)}), bf16[16,8,4,128,128]{4,3,2,0,1:T(8,128)(2,1)}, u32[]{:S(2)}, u32[]{:S(2)}) async-start(bf16[16,8,4,128,128]{4,3,2,0,1:T(8,128)(2,1)} %copy.38), calls=%async_computation | async-start | bytes 33554432 | tf_op jit(solution)/shard_map/all_to_all | solution.py:328

commit v3 on v2

--- a/solution.py
+++ b/solution.py
@@ -11,38 +11,38 @@
 QUAD = 4
 
 
-def pick_kernel(index_ref, spot_ref, got_ref, left_ref, right_ref):
+def pick_kernel(index_ref, spot_ref, got_ref, *refs):
+    left_ref, right_ref = refs[-2:]
     block = got_ref[0]
     left_ref[0, 0] = block
     right_ref[0, 0] = block
 
 
-def pick_rows(index, spot, got, cols, groups):
+def pick_rows(index, spot, got, shapes, half, tables):
     height = index.shape[0]
     block = got.shape[1:]
+    anywhere = pl.BlockSpec(memory_space=pl.ANY)
     return pl.pallas_call(
         pick_kernel,
-        out_shape=(
-            jax.ShapeDtypeStruct((cols, height) + block, got.dtype),
-            jax.ShapeDtypeStruct((groups, height) + block, got.dtype),
-        ),
+        out_shape=shapes,
         grid_spec=pltpu.PrefetchScalarGridSpec(
             num_scalar_prefetch=2,
             grid=(height,),
             in_specs=[
                 pl.BlockSpec((1,) + block, lambda i, index, spot: (index[i], 0, 0, 0)),
-            ],
+            ] + [anywhere] * len(tables),
             out_specs=(
-                pl.BlockSpec((1, 1) + block, lambda i, index, spot: (spot[0], i, 0, 0, 0)),
-                pl.BlockSpec((1, 1) + block, lambda i, index, spot: (spot[1], i, 0, 0, 0)),
+                pl.BlockSpec((1, 1) + block, lambda i, index, spot: (spot[0], i, half, 0, 0)),
+                pl.BlockSpec((1, 1) + block, lambda i, index, spot: (spot[1], i, half, 0, 0)),
             ),
         ),
+        input_output_aliases={3: 0, 4: 1} if tables else {},
         name="pick_rows",
-    )(index, spot, got)
+    )(index, spot, got, *tables)
 
 
 def spread_kernel(
-    rows, cols, layers, outer, parts, left_in, right_in, left_ref, right_ref,
+    rows, cols, layers, outer, parts, panels, left_in, right_in, left_ref, right_ref,
     send_sem, recv_sem, row_send, layer_send, table_recv,
 ):
     inner = cols // outer
@@ -77,7 +77,7 @@
 
     def send_left(kind, part, item, way, condition):
         def make():
-            place = left_ref.at[item, part]
+            place = left_ref.at[item, part, panels]
             return pltpu.make_async_remote_copy(
                 src_ref=place,
                 dst_ref=place,
@@ -98,7 +98,7 @@
     def wait_left(kind, part, item, condition):
         @pl.when(condition)
         def _():
-            place = left_ref.at[item, part]
+            place = left_ref.at[item, part, panels]
             pltpu.make_async_remote_copy(
                 src_ref=place,
                 dst_ref=place,
@@ -153,8 +153,8 @@
 
     def row_copy(d, peer):
         return pltpu.make_async_remote_copy(
-            src_ref=right_ref.at[my_group],
-            dst_ref=right_ref.at[my_group],
+            src_ref=right_ref.at[my_group, :, panels],
+            dst_ref=right_ref.at[my_group, :, panels],
             send_sem=row_send.at[d],
             recv_sem=table_recv.at[my_group],
             device_id={"row": peer},
@@ -164,8 +164,8 @@
     def layer_copy(d, peer, row):
         group = row * layers + my_layer
         return pltpu.make_async_remote_copy(
-            src_ref=right_ref.at[group],
-            dst_ref=right_ref.at[group],
+            src_ref=right_ref.at[group, :, panels],
+            dst_ref=right_ref.at[group, :, panels],
             send_sem=layer_send.at[d, row],
             recv_sem=table_recv.at[group],
             device_id={"layer": peer},
@@ -174,8 +174,8 @@
 
     def wait_table(group):
         pltpu.make_async_remote_copy(
-            src_ref=right_ref.at[group],
-            dst_ref=right_ref.at[group],
+            src_ref=right_ref.at[group, :, panels],
+            dst_ref=right_ref.at[group, :, panels],
             send_sem=row_send.at[0],
             recv_sem=table_recv.at[group],
             device_id={"row": my_row},
@@ -212,17 +212,19 @@
             layer_copy(d, peer, row).wait_send()
 
 
-def spread(left, right, rows, cols, layers):
+def spread(left, right, rows, cols, layers, half, halves):
     outer = 4 if cols % 4 == 0 else 1
     height = left.shape[1]
-    swapped = max(height // 8, 1)
+    swapped = max(height * 10 // 64, 1)
+    chunk = left.shape[2] // halves
+    panels = pl.ds(half * chunk, chunk)
     count = min(4, height - swapped)
     cuts = [swapped + (height - swapped) * k // count for k in range(count + 1)]
     parts = [(0, swapped, False)]
     parts += [(lo, hi - lo, True) for lo, hi in zip(cuts, cuts[1:])]
     kinds = len(parts)
     return pl.pallas_call(
-        functools.partial(spread_kernel, rows, cols, layers, outer, tuple(parts)),
+        functools.partial(spread_kernel, rows, cols, layers, outer, tuple(parts), panels),
         out_shape=(
             jax.ShapeDtypeStruct(left.shape, left.dtype),
             jax.ShapeDtypeStruct(right.shape, right.dtype),
@@ -237,7 +239,10 @@
             pltpu.SemaphoreType.DMA((layers, rows)),
             pltpu.SemaphoreType.DMA((rows * layers,)),
         ],
-        compiler_params=pltpu.CompilerParams(collective_id=0, has_side_effects=True),
+        compiler_params=pltpu.CompilerParams(collective_id=half, has_side_effects=True),
+        cost_estimate=pl.CostEstimate(
+            flops=0, bytes_accessed=1 << 30, transcendentals=0
+        ),
         name="spread",
     )(left, right)
 
@@ -324,12 +329,6 @@
 
     ids = jnp.concatenate([slot_rows[:, None], block_cols], axis=1)
     ids = lax.all_gather(ids, ("row", "col", "layer"), axis=0, tiled=True)
-    owned_blocks, ids = lax.optimization_barrier((owned_blocks, ids))
-    got = lax.all_to_all(
-        owned_blocks.reshape(own_slots, cols, width, size, size),
-        "col", split_axis=1, concat_axis=0, tiled=True,
-    ).reshape(cols * own_slots, width, size, size)
-
     nb = NB
     per_layer = panels // (cols * layers) * (nb // panels)
     height = nb // (rows * layers)
@@ -347,12 +346,28 @@
     )
     my_slots = lax.dynamic_slice_in_dim(slot_at, my_group * height, height)
     owner = my_slots // own_slots // layers % cols
-    left, right = pick_rows(
-        owner * own_slots + my_slots % own_slots,
-        jnp.stack([my_col, my_group]).astype(jnp.int32),
-        got, cols, rows * layers,
-    )
-    left, right = spread(left, right, rows, cols, layers)
+    index = owner * own_slots + my_slots % own_slots
+    spot = jnp.stack([my_col, my_group]).astype(jnp.int32)
+    shapes = (
+        jax.ShapeDtypeStruct((cols, height, width, size, size), owned_blocks.dtype),
+        jax.ShapeDtypeStruct((rows * layers, height, width, size, size), owned_blocks.dtype),
+    )
+    halves = 2 if width % 2 == 0 else 1
+    chunk = width // halves
+    owned = owned_blocks.reshape(own_slots, cols, width, size, size)
+    owned, ids = lax.optimization_barrier((owned, ids))
+    arrived = []
+    for half in range(halves):
+        piece = owned[:, :, half * chunk:(half + 1) * chunk]
+        if arrived:
+            piece, arrived[-1] = lax.optimization_barrier((piece, arrived[-1]))
+        got = lax.all_to_all(piece, "col", split_axis=1, concat_axis=0, tiled=True)
+        arrived.append(got.reshape(cols * own_slots, chunk, size, size))
+    tables = ()
+    for half in range(halves):
+        tables = pick_rows(index, spot, arrived[half], shapes, half, tables)
+        tables = spread(*tables, rows, cols, layers, half, halves)
+    left, right = tables
 
     columns = jnp.dot(
         holds.astype(jnp.float32),

time: 1250 us -> 1180 us (0.944)
  waiting for transfers between devices: 352 us -> 0.01 us
  blocking collectives: 43.9 us -> 231 us
  Pallas kernels: 815 us -> 917 us
    all_to_all x1, waiting for transfers between devices: 352 us -> 0.01 us  [shards(): got = lax.all_to_all(piece, 'col', split_axis=1, concat_axis=0, tiled=True)]
    all_to_all x0 -> x1, blocking collectives: none -> 187 us  [shards(): got = lax.all_to_all(piece, 'col', split_axis=1, concat_axis=0, tiled=True)]
    pallas_call x1 -> x2, Pallas kernels: 657 us -> 729 us  [spread(): pl.pallas_call(functools.partial(spread_kernel, rows, cols, layers, outer...]
    pallas_call x1 -> x2, Pallas kernels: 36.8 us -> 67.4 us  [pick_rows(): pl.pallas_call(pick_kernel, out_shape=shapes, grid_spec=pltpu.PrefetchSca...]
    reshape x1 -> x0, local copies, waits for them, and re-layouts: 14.1 us -> none  [shards(): owned_blocks.reshape(own_slots, cols, width, size, size)]
  transfers between devices with their start and end apart: 1 -> 1, of which waited for: 1 -> 0; matrix products, arithmetic and copies ran while one was open for 1% -> 1% of each run, Pallas kernels for 0% -> 37%
where the time goes in v3:
time: 1180 us
  Pallas kernels  917 us (78%)
  blocking collectives  231 us (20%)
  local copies, waits for them, and re-layouts  17.5 us (1%)
    pallas_call x2, Pallas kernels, spread(): pl.pallas_call(functools.partial(spread_kernel, rows, cols, layers, outer...  729 us
    all_to_all x1, blocking collectives, shards(): got = lax.all_to_all(piece, 'col', split_axis=1, concat_axis=0, tiled=True)  187 us
    pallas_call x1, Pallas kernels, multiply(): pl.pallas_call(multiply_kernel, out_shape=jax.ShapeDtypeStruct((height, w...  120 us
    pallas_call x2, Pallas kernels, pick_rows(): pl.pallas_call(pick_kernel, out_shape=shapes, grid_spec=pltpu.PrefetchSca...  67.4 us
    all_gather x1, blocking collectives, shards(): ids = lax.all_gather(ids, ('row', 'col', 'layer'), axis=0, tiled=True)  43.9 us
  transfers between devices with their start and end apart: 1, of which 0 were waited for; matrix products, arithmetic and copies ran while one was open for 1% of the time, Pallas kernels for 37%

profile of v3, /device:TPU:0, one launch (start us, length us, event | category | flops | bytes accessed | tf_op | source)
XLA Modules:
  0.0 1175.2 jit_solution(11995594102731994627)
XLA Ops:
  0.0 0.7 copy.37
  0.7 0.8 pad_add_fusion
  1.5 43.9 %all_gather.3 = s32[512,33]{1,0:T(8,128)S(1)} all-gather(s32[16,33]{1,0:T(8,128)S(1)} %pad_add_fusion), channel_id=1, replica_groups=mesh['row'=2,'col'=8,'layer'=2] {'row','col','layer'}, dimensions={0}, use_global_device_ids=true | all-gather | bytes 69696 | tf_op jit(solution)/shard_map/all_gather | solution.py:331
  45.4 9.6 fusion.30
  55.0 187.2 %all_to_all.30 = bf16[16,8,2,128,128]{4,3,2,0,1:T(8,128)(2,1)} all-to-all(bf16[16,8,2,128,128]{4,3,2,0,1:T(8,128)(2,1)S(1)} %get-tuple-element.33), channel_id=1, replica_groups=mesh['row'=2,'col'=8,'layer'=2] {'col'}, dimensions={1} | all-to-all | bytes 16777216 | tf_op jit(solution)/shard_map/all_to_all | solution.py:364
  242.2 4.9 all-to-all-start.1
  247.2 0.1 slice_reduce_fusion
  247.4 0.5 convolution_convert_fusion
  247.9 0.1 compare_select_fusion.1
  248.0 0.1 copy.38
  248.1 0.1 reshape.122
  248.2 0.1 copy.39
  248.3 5.5 gather_fusion
  253.8 0.5 copy.40
  254.3 0.1 dynamic_slice.14
  254.4 0.2 convert_reduce_fusion
  254.6 0.1 copy.41
  254.8 0.1 copy.44
  254.9 0.1 sub.71
  255.0 0.8 reduce_window_sum.11
  255.8 0.1 copy.42
  255.9 0.1 add_add_fusion
  256.0 0.6 select_reduce_fusion
  256.6 0.1 copy.43
  256.7 0.1 add.173.pair_ref
  256.9 0.2 fusion.2
  257.1 0.7 fusion.26.index_ref
  257.8 0.7 pad_add_fusion.1.spot_ref
  258.4 33.7 %pick_rows.2 = (bf16[8,64,4,128,128]{4,3,2,1,0:T(8,128)(2,1)}, bf16[4,64,4,128,128]{4,3,2,1,0:T(8,128)(2,1)}) custom-call(s32[64]{0:T(128)} %fusion.26.index_ref, s32[2]{0:T(128)} %pad_add_fusion.1.spot_ref, bf16[128,2,128,128]{3,2,1,0:T(8,128)(2,1)} %bitcast.20), custom_call_target="tpu_custom_call" | custom-call | tf_op jit(solution)/shard_map/pick_rows/pallas_call | solution.py:25
  292.1 406.2 %spread.2 = (bf16[8,64,4,128,128]{4,3,2,1,0:T(8,128)(2,1)}, bf16[4,64,4,128,128]{4,3,2,1,0:T(8,128)(2,1)}) custom-call(bf16[8,64,4,128,128]{4,3,2,1,0:T(8,128)(2,1)} %get-tuple-element.21.left_in, bf16[4,64,4,128,128]{4,3,2,1,0:T(8,128)(2,1)} %get-tuple-element.22.right_in), custom_call_target="tpu_custom_call", output_to_operand_aliasing={{0}: (0, {}), {1}: (1, {})} | custom-call | bytes 1073741824 | tf_op jit(solution)/shard_map/spread/pallas_call | solution.py:226
  698.3 0.0 all-to-all-done.1
  698.4 33.7 %pick_rows.3 = (bf16[8,64,4,128,128]{4,3,2,1,0:T(8,128)(2,1)}, bf16[4,64,4,128,128]{4,3,2,1,0:T(8,128)(2,1)}) custom-call(s32[64]{0:T(128)} %fusion.26.index_ref, s32[2]{0:T(128)} %pad_add_fusion.1.spot_ref, bf16[128,2,128,128]{3,2,1,0:T(8,128)(2,1)} %bitcast.11.got_ref, ...), custom_call_target="tpu_custom_call", output_to_operand_aliasing={{0}: (3, {}), {1}: (4, {})} | custom-call | tf_op jit(solution)/shard_map/pick_rows/pallas_call | solution.py:25
  732.0 323.0 %spread.3 = (bf16[8,64,4,128,128]{4,3,2,1,0:T(8,128)(2,1)}, bf16[4,64,4,128,128]{4,3,2,1,0:T(8,128)(2,1)}) custom-call(bf16[8,64,4,128,128]{4,3,2,1,0:T(8,128)(2,1)} %get-tuple-element.25.left_in, bf16[4,64,4,128,128]{4,3,2,1,0:T(8,128)(2,1)} %get-tuple-element.26.right_in), custom_call_target="tpu_custom_call", output_to_operand_aliasing={{0}: (0, {}), {1}: (1, {})} | custom-call | bytes 1073741824 | tf_op jit(solution)/shard_map/spread/pallas_call | solution.py:226
  1055.0 120.2 %multiply.3 = bf16[64,4,128,128]{3,2,1,0:T(8,128)(2,1)} custom-call(s32[8192]{0:T(1024)S(1)} %add.173.pair_ref, s32[256]{0:T(256)S(1)} %and_select_fusion.4.turns_ref, bf16[8,64,4,128,128]{4,3,2,1,0:T(8,128)(2,1)} %get-tuple-element.27.left_ref, bf16[256,4,128,128]{3,2,1,0:T(8,128)(2,1)} %bitcast.19), custom_call_target="tpu_custom_call" | custom-call | tf_op jit(solution)/shard_map/multiply/pallas_call | solution.py:299
  (9 shorter events, 0.1 us)
Async XLA Ops:
  242.2 456.1 %all-to-all-start.1 = ((bf16[16,8,2,128,128]{4,3,2,0,1:T(8,128)(2,1)}), bf16[16,8,2,128,128]{4,3,2,0,1:T(8,128)(2,1)}, u32[]{:S(2)}, u32[]{:S(2)}) async-start(bf16[16,8,2,128,128]{4,3,2,0,1:T(8,128)(2,1)} %get-tuple-element.19), calls=%async_computation.1 | async-start | bytes 16777216 | tf_op jit(solution)/shard_map/all_to_all | solution.py:364
